TPU v7x, 128 devices: a whole 4x4x4 slice. The times are simulated.
128 devices in a mesh: req: 32 (over y, z, core), grp: 4 (over x).
Axes of the slice: x: 4, y: 4, z: 4, core: 2. Of those that a mesh axis runs over, the one named last changes fastest.
Arguments:
- hidden_in: bfloat16 [16384, 2048], P('req'), may hold values from -6 to 6
- attn_gain: float32 [2048], replicated, may hold values from 0.1 to 1.9
- mlp_gain: float32 [2048], replicated, may hold values from 0.1 to 1.9
- w_query: bfloat16 [2048, 2048], P(None, 'grp'), may hold values from -0.75 to 0.75
- w_key: bfloat16 [2048, 512], P(None, 'grp'), may hold values from -0.125 to 0.125
- w_value: bfloat16 [2048, 512], P(None, 'grp'), may hold values from -0.125 to 0.125
- w_out: bfloat16 [2048, 2048], P('grp'), may hold values from -0.125 to 0.125
- w_gate: bfloat16 [2048, 8192], P(None, 'req'), may hold values from -0.125 to 0.125
- w_up: bfloat16 [2048, 8192], P(None, 'req'), may hold values from -0.125 to 0.125
- w_down: bfloat16 [8192, 2048], P('req'), may hold values from -0.0625 to 0.0625
- cache_k: bfloat16 [16384, 16, 512], P('req', None, 'grp'), may hold values from -4000 to 4000
- cache_v: bfloat16 [16384, 16, 512], P('req', None, 'grp'), may hold values from -6 to 6
- owner_of_row: int32 [16384], P('req'), may hold values from 0 to 31, as said below
- new_len: int32 [32, 32], P('req'), may hold values from 0 to 32, as said below
- prior_len: int32 [32, 32], P('req'), may hold values from 0 to 256, as said below
- page_table: int32 [32, 512], P('req'), may hold values from 0 to 511, each once within a row
Outputs:
- layer_out: bfloat16 [16384, 2048], P(('req', 'grp'))
- new_cache_k: bfloat16 [16384, 16, 512], P('req', None, 'grp')
- new_cache_v: bfloat16 [16384, 16, 512], P('req', None, 'grp')
Inputs may be any that keep to these rules, and one draw needn't show every extreme that they name: `owner_of_row`: rows of one block of 512 that name the same owner are consecutive; each block holds at most one request for each owner, of at most 32 rows; in every draw one owner receives a request of exactly 32 rows from every block. new_len[o, s] is the number of rows of block s of owner_of_row that name o. prior_len[o, s] + new_len[o, s] <= 256.
All inputs are finite; a program needn't handle non-finite values.
Results may differ from a plain program's by a relative error of at most 0.0063.
Values may be sent and summed in bfloat16 or wider, within the bound.
A program may use at most 128 MiB of HBM per device.

v0:
```python
import jax
import jax.numpy as jnp
from jax import lax
from jax.sharding import PartitionSpec as P

HD = 64
PAGE = 16
MAXP = 16
CONTEXT = 256
EPSILON = 1e-05
RESIDUAL_MULT = 0.22
SCORE_MULT = 0.015625
ROPE_BASE = 10000000.0


def normalize(values, gain):
    mean_square = jnp.mean(values * values, axis=-1, keepdims=True)
    return values * lax.rsqrt(mean_square + EPSILON) * gain


def rotary(values, positions):
    dim = values.shape[-1]
    half = dim // 2
    freq = jnp.power(ROPE_BASE, -2.0 * jnp.arange(half, dtype=jnp.int32).astype(jnp.float32) / dim)
    angle = positions.astype(jnp.float32)[:, :, None] * freq
    cosine = jnp.cos(angle)[:, :, None, :]
    sine = jnp.sin(angle)[:, :, None, :]
    first = values[..., :half].astype(jnp.float32)
    second = values[..., half:].astype(jnp.float32)
    return jnp.concatenate(
        [first * cosine - second * sine, second * cosine + first * sine], axis=-1
    )


def source_layout(owner_block, peers, pair_rows):
    row_count = owner_block.shape[0]
    owners = jnp.arange(peers, dtype=jnp.int32)
    member = owner_block[None, :] == owners[:, None]
    counts = jnp.sum(member.astype(jnp.int32), axis=1)
    row_ids = jnp.arange(row_count, dtype=jnp.int32)
    starts = jnp.min(jnp.where(member, row_ids[None, :], row_count), axis=1)
    slots = jnp.arange(pair_rows, dtype=jnp.int32)
    gather_rows = jnp.where(
        slots[None, :] < counts[:, None], starts[:, None] + slots[None, :], row_count
    )
    row_start = jnp.sum(jnp.where(member, starts[:, None], 0), axis=0)
    back_rows = owner_block * pair_rows + (row_ids - row_start)
    return (gather_rows.reshape(-1), back_rows)


def owner_attention(query_in, key_in, value_in, cache_keys, cache_values, lengths, priors, table):
    sources, pair_rows, qcols = query_in.shape
    kcols = key_in.shape[-1]
    kv_heads = kcols // HD
    group = qcols // kcols
    pool_pages = cache_keys.shape[0]
    slots = jnp.arange(pair_rows, dtype=jnp.int32)
    positions = priors[:, None] + slots[None, :]
    live = slots[None, :] < lengths[:, None]
    query_rot = rotary(query_in.reshape(sources, pair_rows, qcols // HD, HD), positions).astype(
        jnp.bfloat16
    )
    key_rot = rotary(key_in.reshape(sources, pair_rows, kv_heads, HD), positions).astype(
        jnp.bfloat16
    )
    key_rot = key_rot.reshape(sources, pair_rows, kcols)
    pages = table.reshape(sources, MAXP)
    page_index = jnp.minimum(positions // PAGE, MAXP - 1)
    target = jnp.take_along_axis(pages, page_index, axis=1)
    target = jnp.where(live, target, pool_pages).reshape(-1)
    offset = (positions % PAGE).reshape(-1)
    keys_out = cache_keys.at[target, offset].set(key_rot.reshape(-1, kcols), mode="drop")
    values_out = cache_values.at[target, offset].set(value_in.reshape(-1, kcols), mode="drop")
    key_block = jnp.take(keys_out, pages.reshape(-1), axis=0).reshape(
        sources, CONTEXT, kv_heads, HD
    )
    value_block = jnp.take(values_out, pages.reshape(-1), axis=0).reshape(
        sources, CONTEXT, kv_heads, HD
    )
    grouped = query_rot.reshape(sources, pair_rows, kv_heads, group, HD)
    scores = (
        jnp.einsum("stkgd,sjkd->skgtj", grouped, key_block, preferred_element_type=jnp.float32)
        * SCORE_MULT
    )
    allowed = (
        jnp.arange(CONTEXT, dtype=jnp.int32)[None, None, None, None, :]
        <= positions[:, None, None, :, None]
    )
    scores = jnp.where(allowed, scores, -jnp.inf)
    top = jnp.max(scores, axis=-1, keepdims=True)
    weights = jnp.exp(scores - top)
    probs = (weights / jnp.sum(weights, axis=-1, keepdims=True)).astype(jnp.bfloat16)
    mixed = jnp.einsum("skgtj,sjkd->stkgd", probs, value_block, preferred_element_type=jnp.float32)
    return (mixed.astype(jnp.bfloat16).reshape(sources, pair_rows, qcols), keys_out, values_out)


def body(
    hidden_in,
    attn_gain,
    mlp_gain,
    w_query,
    w_key,
    w_value,
    w_out,
    w_gate,
    w_up,
    w_down,
    cache_k,
    cache_v,
    owner_of_row,
    new_len,
    prior_len,
    page_table,
):
    peers = lax.axis_size("req")
    groups = lax.axis_size("grp")
    row_count = hidden_in.shape[0]
    pair_rows = 2 * row_count // peers
    quarter = row_count // groups
    group_index = lax.axis_index("grp")
    normed = normalize(hidden_in.astype(jnp.float32), attn_gain).astype(jnp.bfloat16)
    query_rows = jnp.dot(normed, w_query, preferred_element_type=jnp.float32).astype(jnp.bfloat16)
    key_rows = jnp.dot(normed, w_key, preferred_element_type=jnp.float32).astype(jnp.bfloat16)
    value_rows = jnp.dot(normed, w_value, preferred_element_type=jnp.float32).astype(jnp.bfloat16)
    gather_rows, back_rows = source_layout(owner_of_row, peers, pair_rows)
    send_query = jnp.take(query_rows, gather_rows, axis=0, mode="fill", fill_value=0).reshape(
        peers, pair_rows, -1
    )
    send_key = jnp.take(key_rows, gather_rows, axis=0, mode="fill", fill_value=0).reshape(
        peers, pair_rows, -1
    )
    send_value = jnp.take(value_rows, gather_rows, axis=0, mode="fill", fill_value=0).reshape(
        peers, pair_rows, -1
    )
    recv_query, recv_key, recv_value = (
        lax.all_to_all(send_query, "req", split_axis=0, concat_axis=0, tiled=True),
        lax.all_to_all(send_key, "req", split_axis=0, concat_axis=0, tiled=True),
        lax.all_to_all(send_value, "req", split_axis=0, concat_axis=0, tiled=True),
    )
    mixed, keys_out, values_out = owner_attention(
        recv_query, recv_key, recv_value, cache_k, cache_v, new_len[0], prior_len[0], page_table[0]
    )
    returned = lax.all_to_all(mixed, "req", split_axis=0, concat_axis=0, tiled=True)
    attn_rows = jnp.take(returned.reshape(peers * pair_rows, -1), back_rows, axis=0)
    projected = jnp.dot(attn_rows, w_out, preferred_element_type=jnp.float32)
    total = lax.psum(projected.astype(jnp.bfloat16), "grp").astype(jnp.float32)
    attn_part = lax.dynamic_slice_in_dim(total, group_index * quarter, quarter, 0)
    own_rows = lax.dynamic_slice_in_dim(hidden_in, group_index * quarter, quarter, 0).astype(
        jnp.float32
    )
    residual = own_rows + RESIDUAL_MULT * attn_part
    mlp_in = normalize(residual, mlp_gain).astype(jnp.bfloat16)
    piece = lax.all_gather(mlp_in, "req", axis=0, tiled=True)
    gate = jnp.dot(piece, w_gate, preferred_element_type=jnp.float32)
    upper = jnp.dot(piece, w_up, preferred_element_type=jnp.float32)
    hidden = (jax.nn.silu(gate) * upper).astype(jnp.bfloat16)
    down = lax.psum_scatter(
        jnp.dot(hidden, w_down, preferred_element_type=jnp.float32).astype(jnp.bfloat16),
        "req",
        scatter_dimension=0,
        tiled=True,
    ).astype(jnp.float32)
    layer_out = (residual + RESIDUAL_MULT * down).astype(jnp.bfloat16)
    return (layer_out, keys_out, values_out)


def solution(mesh):
    in_specs = (
        P("req", None),
        P(),
        P(),
        P(None, "grp"),
        P(None, "grp"),
        P(None, "grp"),
        P("grp", None),
        P(None, "req"),
        P(None, "req"),
        P("req", None),
        P("req", None, "grp"),
        P("req", None, "grp"),
        P("req"),
        P("req", None),
        P("req", None),
        P("req", None),
    )
    out_specs = (P(("req", "grp"), None), P("req", None, "grp"), P("req", None, "grp"))
    return jax.shard_map(body, mesh=mesh, in_specs=in_specs, out_specs=out_specs, check_vma=False)
```

profile of v0, /device:TPU:0, one launch (start us, length us, event | category | flops | bytes accessed | tf_op | source)
XLA Modules:
  0.0 475.2 jit_solution(9839665422419617770)
XLA Ops:
  7.2 3.4 copy.67
  18.9 3.2 gather_fusion.5
  22.1 3.2 gather_fusion.3
  26.3 8.4 %all-to-all-start.1 = ((bf16[32,32,128]{2,1,0:T(8,128)(2,1)}), bf16[32,32,128]{2,1,0:T(8,128)(2,1)S(1)}, u32[]{:S(2)}, u32[]{:S(2)}) async-start(bf16[32,32,128]{2,1,0:T(8,128)(2,1)} %bitcast.10), calls=%async_computation.1 | async-start | bytes 524288 | tf_op jit(solution)/shard_map/all_to_all | solution.py:137
  37.1 7.1 %gather_fusion.2 = s32[1024]{0:T(1024)S(1)} fusion(s32[32,16]{1,0:T(8,128)S(1)} %reshape_squeeze.3, s32[1024]{0:T(1024)S(1)} %reshape.573), kind=kCustom, calls=%fused_computation.6 | custom fusion | bytes 16384 | tf_op jit(solution)/shard_map/jit(take_along_axis)/gather | solution.py:69
  44.4 3.5 convolution_convert_fusion.2
  48.0 5.1 %gather_fusion = bf16[1024,512]{1,0:T(8,128)(2,1)} fusion(bf16[512,512]{1,0:T(8,128)(2,1)S(1)} %convolution_convert_fusion.2, s32[1024]{0:T(1024)S(1)} %broadcast_clamp_fusion), kind=kCustom, calls=%fused_computation.4 | custom fusion | bytes 2101248 | tf_op jit(solution)/shard_map/jit(_take)/gather | solution.py:126
  56.4 7.5 %all-to-all-start = ((bf16[32,32,128]{2,1,0:T(8,128)(2,1)}), bf16[32,32,128]{2,1,0:T(8,128)(2,1)}, u32[]{:S(2)}, u32[]{:S(2)}) async-start(bf16[32,32,128]{2,1,0:T(8,128)(2,1)} %bitcast.5), calls=%async_computation | async-start | bytes 524288 | tf_op jit(solution)/shard_map/all_to_all | solution.py:138
  63.9 2.9 multiply_cosine_fusion
  67.1 5.7 %all-to-all-done = bf16[32,32,128]{2,1,0:T(8,128)(2,1)} async-done(((bf16[32,32,128]{2,1,0:T(8,128)(2,1)}), bf16[32,32,128]{2,1,0:T(8,128)(2,1)}, u32[]{:S(2)}, u32[]{:S(2)}) %all-to-all-start) | async-done | bytes 262176 | tf_op jit(solution)/shard_map/all_to_all | solution.py:138
  72.9 5.1 %all-to-all-start.2 = ((bf16[32,32,512]{2,1,0:T(8,128)(2,1)}), bf16[32,32,512]{2,1,0:T(8,128)(2,1)}, u32[]{:S(2)}, u32[]{:S(2)}) async-start(bf16[32,32,512]{2,1,0:T(8,128)(2,1)} %broadcast_select_fusion.2), calls=%async_computation.2 | async-start | bytes 2097152 | tf_op jit(solution)/shard_map/all_to_all | solution.py:136
  81.6 6.5 %scatter_fusion.1 = bf16[8192,128]{1,0:T(8,128)(2,1)} fusion(bf16[8192,128]{1,0:T(8,128)(2,1)} %bitcast.52, s32[1024]{0:T(1024)S(1)} %broadcast_select_fusion.5, bf16[1024,128]{1,0:T(8,128)(2,1)S(1)} %reshape.587), kind=kCustom, calls=%fused_computation.8 | custom fusion | bytes 790528
  88.0 4.0 gather_fusion.6
  92.0 6.9 %scatter_fusion = bf16[8192,128]{1,0:T(8,128)(2,1)} fusion(bf16[8192,128]{1,0:T(8,128)(2,1)} %bitcast.49, s32[1024]{0:T(1024)S(1)} %broadcast_select_fusion.5, bf16[1024,128]{1,0:T(8,128)(2,1)} %bitcast.6), kind=kCustom, calls=%fused_computation.7 | custom fusion | bytes 790528
  98.9 4.0 gather_fusion.4
  102.9 4.6 broadcast_select_fusion.1
  107.5 8.2 %reshape.510 = bf16[32,256,2,64]{3,2,1,0:T(2,128)(2,1)} reshape(bf16[512,16,128]{2,1,0:T(8,128)(2,1)} %get-tuple-element.22) | data formatting | bytes 4194304 | tf_op jit(solution)/shard_map/reshape | solution.py:77
  115.7 8.3 %reshape.513 = bf16[32,256,2,64]{3,2,1,0:T(2,128)(2,1)} reshape(bf16[512,16,128]{2,1,0:T(8,128)(2,1)} %get-tuple-element.23) | data formatting | bytes 4194304 | tf_op jit(solution)/shard_map/reshape | solution.py:74
  124.0 3.9 reshape.514
  127.9 4.0 fusion.7
  135.8 4.9 %fusion.49 = (f32[32,2,4,32]{3,2,1,0:T(4,128)S(1)}, f32[32,2,4,32,256]{4,3,2,1,0:T(8,128)}) fusion(f32[32,2,256,32,4]{2,3,4,1,0:T(8,128)S(1)} %fusion.10, pred[32,32,256]{2,1,0:T(8,128)(4,1)S(1)} %copy-done.6), kind=kOutput, calls=%fused_computation.132 | output fusion | flops 12583167 | bytes 17072128 | tf_op jit(solution)/shard_map/sub | solution.py:91
  140.7 4.5 convert_bitcast_fusion
  147.7 4.7 reshape.515
  152.4 7.5 %all-to-all-start.3 = ((bf16[32,32,512]{2,1,0:T(8,128)(2,1)}), bf16[32,32,512]{2,1,0:T(8,128)(2,1)S(1)}, u32[]{:S(2)}, u32[]{:S(2)}) async-start(bf16[32,32,512]{2,1,0:T(8,128)(2,1)} %reshape.515), calls=%async_computation.3 | async-start | bytes 2097152 | tf_op jit(solution)/shard_map/all_to_all | solution.py:143
  159.9 16.7 %all-to-all-done.3 = bf16[32,32,512]{2,1,0:T(8,128)(2,1)S(1)} async-done(((bf16[32,32,512]{2,1,0:T(8,128)(2,1)}), bf16[32,32,512]{2,1,0:T(8,128)(2,1)S(1)}, u32[]{:S(2)}, u32[]{:S(2)}) %all-to-all-start.3) | async-done | bytes 1048608 | tf_op jit(solution)/shard_map/all_to_all | solution.py:143
  176.7 2.6 gather_fusion.1
  179.3 3.7 convolution_convert_fusion.1
  183.1 56.8 %all-reduce.2.cloned.1.call-done = bf16[512,2048]{1,0:T(8,128)(2,1)} async-done(((bf16[512,2048]{1,0:T(8,128)(2,1)}), bf16[512,2048]{1,0:T(8,128)(2,1)}) %all-reduce.2.cloned.1.call-update) | async-done | bytes 2097168 | tf_op jit(solution)/shard_map/psum | solution.py:146
  243.7 72.5 %all-gather.2.cloned.1.call-done = bf16[4096,2048]{1,0:T(8,128)(2,1)} async-done(((bf16[128,2048]{1,0:T(8,128)(2,1)}), bf16[4096,2048]{1,0:T(8,128)(2,1)}) %all-gather.2.cloned.1.call-update) | async-done | bytes 16777232 | tf_op jit(solution)/shard_map/all_gather | solution.py:153
  316.2 10.2 %fusion.50 = f32[4096,256]{1,0:T(8,128)} fusion(bf16[4096,2048]{1,0:T(8,128)(2,1)} %all-gather.2.cloned.1.call-done, bf16[2048,256]{1,0:T(8,128)(2,1)S(1)} %copy-done.14), kind=kOutput, calls=%fused_computation.133 | convolution fusion | flops 4294967296 | bytes 22020096 | tf_op jit(solution)/shard_map/dot_general | solution.py:154
  326.4 24.7 %convolution_convert_fusion = bf16[4096,2048]{1,0:T(8,128)(2,1)} fusion(bf16[256,2048]{1,0:T(8,128)(2,1)} %param.29, bf16[4096,2048]{1,0:T(8,128)(2,1)} %all-gather.2.cloned.1.call-done, bf16[2048,256]{1,0:T(8,128)(2,1)} %param.28, f32[4096,256]{1,0:T(8,128)} %fusion.50), kind=kOutput, calls=%fused_computation.10 | convolution fusion | flops 8604614656 | bytes 39845888 | tf_op jit(solution)/shard_map/dot_general | solution.py:158
  351.2 114.9 %reduce-scatter.2.cloned.1.call-done = bf16[128,2048]{1,0:T(8,128)(2,1)} async-done(((bf16[4096,2048]{1,0:T(8,128)(2,1)}), bf16[128,2048]{1,0:T(8,128)(2,1)}) %reduce-scatter.2.cloned.1.call-update) | async-done | bytes 524304 | tf_op jit(solution)/shard_map/reduce_scatter | solution.py:157
  (100 shorter events, 31.5 us)
Async XLA Ops:
  7.2 172.1 %copy-start = (bf16[512,2048]{1,0:T(8,128)(2,1)S(1)}, bf16[512,2048]{1,0:T(8,128)(2,1)}, u32[]{:S(2)}) copy-start(bf16[512,2048]{1,0:T(8,128)(2,1)} %param.26) | copy-start | bytes 6291460
  7.2 3.4 copy-start.5
  7.2 4.8 %copy-start.8 = (s32[512]{0:T(512)S(1)}, s32[512]{0:T(512)}, u32[]{:S(2)}) copy-start(s32[512]{0:T(512)} %param.32) | copy-start | bytes 6148
  10.6 4.0 copy-start.15
  10.6 4.0 copy-start.16
  12.3 4.6 copy-start.2
  18.8 15.9 %copy-start.7 = (s32[1,512]{1,0:T(1,128)S(1)}, s32[1,512]{1,0:T(1,128)}, u32[]{:S(2)}) copy-start(s32[1,512]{1,0:T(1,128)} %param.35) | copy-start | bytes 6148
  18.8 16.0 %copy-start.10 = (s32[1,32]{1,0:T(1,128)S(1)}, s32[1,32]{1,0:T(1,128)}, u32[]{:S(2)}) copy-start(s32[1,32]{1,0:T(1,128)} %param.34) | copy-start | bytes 388
  18.8 17.6 %copy-start.11 = (s32[1,32]{1,0:T(1,128)S(1)}, s32[1,32]{1,0:T(1,128)}, u32[]{:S(2)}) copy-start(s32[1,32]{1,0:T(1,128)} %param.33) | copy-start | bytes 388
  26.3 30.1 %all-to-all-start.1 = ((bf16[32,32,128]{2,1,0:T(8,128)(2,1)}), bf16[32,32,128]{2,1,0:T(8,128)(2,1)S(1)}, u32[]{:S(2)}, u32[]{:S(2)}) async-start(bf16[32,32,128]{2,1,0:T(8,128)(2,1)} %bitcast.10), calls=%async_computation.1 | async-start | bytes 524288 | tf_op jit(solution)/shard_map/all_to_all | solution.py:137
  37.1 7.2 %copy-start.13 = (s32[2]{0:T(128)S(1)}, s32[2]{0:T(128)}, u32[]{:S(2)}) copy-start(s32[2]{0:T(128)} %constant.139) | copy-start | bytes 28
  37.1 7.3 %copy-start.12 = (s32[2]{0:T(128)S(1)}, s32[2]{0:T(128)}, u32[]{:S(2)}) copy-start(s32[2]{0:T(128)} %constant.136) | copy-start | bytes 28
  56.4 16.4 %all-to-all-start = ((bf16[32,32,128]{2,1,0:T(8,128)(2,1)}), bf16[32,32,128]{2,1,0:T(8,128)(2,1)}, u32[]{:S(2)}, u32[]{:S(2)}) async-start(bf16[32,32,128]{2,1,0:T(8,128)(2,1)} %bitcast.5), calls=%async_computation | async-start | bytes 524288 | tf_op jit(solution)/shard_map/all_to_all | solution.py:138
  72.9 51.2 %all-to-all-start.2 = ((bf16[32,32,512]{2,1,0:T(8,128)(2,1)}), bf16[32,32,512]{2,1,0:T(8,128)(2,1)}, u32[]{:S(2)}, u32[]{:S(2)}) async-start(bf16[32,32,512]{2,1,0:T(8,128)(2,1)} %broadcast_select_fusion.2), calls=%async_computation.2 | async-start | bytes 2097152 | tf_op jit(solution)/shard_map/all_to_all | solution.py:136
  115.7 12.2 %copy-start.3 = (f32[32,32,32]{2,1,0:T(8,128)S(1)}, f32[32,32,32]{2,1,0:T(8,128)}, u32[]{:S(2)}) copy-start(f32[32,32,32]{2,1,0:T(8,128)} %get-tuple-element.16) | copy-start | bytes 393220
  131.9 2.2 copy-start.1
  134.1 1.7 copy-start.6
  135.8 4.9 %copy-start.4 = (bf16[32,256,2,64]{3,2,1,0:T(2,128)(2,1)S(1)}, bf16[32,256,2,64]{3,2,1,0:T(2,128)(2,1)}, u32[]{:S(2)}) copy-start(bf16[32,256,2,64]{3,2,1,0:T(2,128)(2,1)} %reshape.510) | copy-start | bytes 6291460
  152.4 24.3 %all-to-all-start.3 = ((bf16[32,32,512]{2,1,0:T(8,128)(2,1)}), bf16[32,32,512]{2,1,0:T(8,128)(2,1)S(1)}, u32[]{:S(2)}, u32[]{:S(2)}) async-start(bf16[32,32,512]{2,1,0:T(8,128)(2,1)} %reshape.515), calls=%async_computation.3 | async-start | bytes 2097152 | tf_op jit(solution)/shard_map/all_to_all | solution.py:143
  159.8 80.0 %all-reduce.2.cloned.1.call-start = ((), (), s32[]{:S(2)}) async-start(), calls=%async_computation.5 | async-start | bytes 4194304 | tf_op jit(solution)/shard_map/psum | solution.py:146
  179.3 62.1 %copy-start.9 = (f32[2048]{0:T(1024)S(1)}, f32[2048]{0:T(1024)}, u32[]{:S(2)}) copy-start(f32[2048]{0:T(1024)} %param.22) | copy-start | bytes 24580
  183.0 133.2 %copy-start.14 = (bf16[2048,256]{1,0:T(8,128)(2,1)S(1)}, bf16[2048,256]{1,0:T(8,128)(2,1)}, u32[]{:S(2)}) copy-start(bf16[2048,256]{1,0:T(8,128)(2,1)} %param.27) | copy-start | bytes 3145732
  183.0 133.2 %all-gather.2.cloned.1.call-start = ((), (), s32[]{:S(2)}) async-start(), calls=%async_computation.6 | async-start | bytes 17301504 | tf_op jit(solution)/shard_map/all_gather | solution.py:153
  243.6 222.4 %reduce-scatter.2.cloned.1.call-start = ((), (), s32[]{:S(2)}) async-start(), calls=%async_computation.7 | async-start | bytes 17301504 | tf_op jit(solution)/shard_map/reduce_scatter | solution.py:157
Sparse Core Ops, SparseCore 0:
  183.1 56.6 all-reduce.1
  243.8 72.4 all-gather.1
  351.3 114.7 reduce-scatter.1
where the time goes:
time: 482 us; the launch traced here: 475 us
  waiting for transfers between devices  267 us (55%)
  local copies, waits for them, and re-layouts  80.5 us (17%)
  matrix products  52.5 us (11%)
  other arithmetic  32.4 us (7%)
  starting transfers between devices  28.7 us (6%)
  between operations  14.4 us (3%)
    reduce_scatter x1, waiting for transfers between devices, body(): lax.psum_scatter(jnp.dot(hidden, w_down, preferred_element_type=jnp.float...  115 us
    all_gather x1, waiting for transfers between devices, body(): piece = lax.all_gather(mlp_in, 'req', axis=0, tiled=True)  72.5 us
    psum x1, waiting for transfers between devices, body(): total = lax.psum(projected.astype(jnp.bfloat16), 'grp').astype(jnp.float32)  56.8 us
    dot_general x1, matrix products, body(): jnp.dot(hidden, w_down, preferred_element_type=jnp.float32)  24.7 us
    unnamed x39, local copies, waits for them, and re-layouts  19.9 us
    all_to_all x1, waiting for transfers between devices, body(): lax.all_to_all(mixed, 'req', split_axis=0, concat_axis=0, tiled=True)  16.7 us
    dot_general x1, matrix products, body(): gate = jnp.dot(piece, w_gate, preferred_element_type=jnp.float32)  10.2 us
  transfers between devices with their start and end apart: 7, of which 5 were waited for; matrix products, arithmetic and copies ran while one was open for 15% of the time, Pallas kernels for 0%

commit v1 on v0

--- a/solution.py
+++ b/solution.py
@@ -143,7 +143,8 @@
     returned = lax.all_to_all(mixed, "req", split_axis=0, concat_axis=0, tiled=True)
     attn_rows = jnp.take(returned.reshape(peers * pair_rows, -1), back_rows, axis=0)
     projected = jnp.dot(attn_rows, w_out, preferred_element_type=jnp.float32)
-    total = lax.psum(projected.astype(jnp.bfloat16), "grp").astype(jnp.float32)
+    meet_the_waves = lambda local, named_axis: jnp.sum(lax.all_gather(local, named_axis), axis=0)
+    total = meet_the_waves(projected.astype(jnp.bfloat16), "grp").astype(jnp.float32)
     attn_part = lax.dynamic_slice_in_dim(total, group_index * quarter, quarter, 0)
     own_rows = lax.dynamic_slice_in_dim(hidden_in, group_index * quarter, quarter, 0).astype(
         jnp.float32

time: 482 us -> 516 us (1.071)
  waiting for transfers between devices: 267 us -> 292 us
  other arithmetic: 32.4 us -> 39.6 us
    all_gather x0 -> x1, waiting for transfers between devices: none -> 81.3 us  [body(): lax.all_gather(local, named_axis)]
    psum x1 -> x0, waiting for transfers between devices: 56.8 us -> none  [body(): total = lax.psum(projected.astype(jnp.bfloat16), 'grp').astype(jnp.float32)]
    reduce_sum x0 -> x1, other arithmetic: none -> 7.24 us  [body(): jnp.sum(lax.all_gather(local, named_axis), axis=0)]
  transfers between devices with their start and end apart: 7 -> 7, of which waited for: 5 -> 5; matrix products, arithmetic and copies ran while one was open for 15% -> 14% of each run, Pallas kernels for 0% -> 0%
where the time goes in v1:
time: 516 us; the launch traced here: 509 us
  waiting for transfers between devices  292 us (57%)
  local copies, waits for them, and re-layouts  80.5 us (16%)
  matrix products  52.7 us (10%)
  other arithmetic  39.6 us (8%)
  starting transfers between devices  28.7 us (6%)
  between operations  14.6 us (3%)
    reduce_scatter x1, waiting for transfers between devices, body(): lax.psum_scatter(jnp.dot(hidden, w_down, preferred_element_type=jnp.float...  115 us
    all_gather x1, waiting for transfers between devices, body(): lax.all_gather(local, named_axis)  81.3 us
    all_gather x1, waiting for transfers between devices, body(): piece = lax.all_gather(mlp_in, 'req', axis=0, tiled=True)  73.7 us
    dot_general x1, matrix products, body(): jnp.dot(hidden, w_down, preferred_element_type=jnp.float32)  24.7 us
    unnamed x39, local copies, waits for them, and re-layouts  19.9 us
    all_to_all x1, waiting for transfers between devices, body(): lax.all_to_all(mixed, 'req', split_axis=0, concat_axis=0, tiled=True)  16.7 us
    dot_general x1, matrix products, body(): gate = jnp.dot(piece, w_gate, preferred_element_type=jnp.float32)  10.4 us
  transfers between devices with their start and end apart: 7, of which 5 were waited for; matrix products, arithmetic and copies ran while one was open for 14% of the time, Pallas kernels for 0%

profile of v1, /device:TPU:0, one launch (start us, length us, event | category | flops | bytes accessed | tf_op | source)
XLA Modules:
  0.0 508.6 jit_solution(1393007268671180222)
XLA Ops:
  7.2 3.4 copy.66
  18.9 3.2 gather_fusion.5
  22.1 3.2 gather_fusion.3
  26.3 8.4 %all-to-all-start.1 = ((bf16[32,32,128]{2,1,0:T(8,128)(2,1)}), bf16[32,32,128]{2,1,0:T(8,128)(2,1)S(1)}, u32[]{:S(2)}, u32[]{:S(2)}) async-start(bf16[32,32,128]{2,1,0:T(8,128)(2,1)} %bitcast.10), calls=%async_computation.1 | async-start | bytes 524288 | tf_op jit(solution)/shard_map/all_to_all | solution.py:137
  37.1 7.1 %gather_fusion.2 = s32[1024]{0:T(1024)S(1)} fusion(s32[32,16]{1,0:T(8,128)S(1)} %reshape_squeeze.3, s32[1024]{0:T(1024)S(1)} %reshape.573), kind=kCustom, calls=%fused_computation.6 | custom fusion | bytes 16384 | tf_op jit(solution)/shard_map/jit(take_along_axis)/gather | solution.py:69
  44.4 3.5 convolution_convert_fusion.2
  48.0 5.1 gather_fusion
  56.4 7.5 %all-to-all-start = ((bf16[32,32,128]{2,1,0:T(8,128)(2,1)}), bf16[32,32,128]{2,1,0:T(8,128)(2,1)}, u32[]{:S(2)}, u32[]{:S(2)}) async-start(bf16[32,32,128]{2,1,0:T(8,128)(2,1)} %bitcast.5), calls=%async_computation | async-start | bytes 524288 | tf_op jit(solution)/shard_map/all_to_all | solution.py:138
  63.9 2.9 multiply_cosine_fusion
  67.1 5.7 %all-to-all-done = bf16[32,32,128]{2,1,0:T(8,128)(2,1)} async-done(((bf16[32,32,128]{2,1,0:T(8,128)(2,1)}), bf16[32,32,128]{2,1,0:T(8,128)(2,1)}, u32[]{:S(2)}, u32[]{:S(2)}) %all-to-all-start) | async-done | bytes 262176 | tf_op jit(solution)/shard_map/all_to_all | solution.py:138
  72.9 5.1 %all-to-all-start.2 = ((bf16[32,32,512]{2,1,0:T(8,128)(2,1)}), bf16[32,32,512]{2,1,0:T(8,128)(2,1)}, u32[]{:S(2)}, u32[]{:S(2)}) async-start(bf16[32,32,512]{2,1,0:T(8,128)(2,1)} %broadcast_select_fusion.2), calls=%async_computation.2 | async-start | bytes 2097152 | tf_op jit(solution)/shard_map/all_to_all | solution.py:136
  81.6 6.5 %scatter_fusion.1 = bf16[8192,128]{1,0:T(8,128)(2,1)} fusion(bf16[8192,128]{1,0:T(8,128)(2,1)} %bitcast.53, s32[1024]{0:T(1024)S(1)} %broadcast_select_fusion.5, bf16[1024,128]{1,0:T(8,128)(2,1)S(1)} %reshape.587), kind=kCustom, calls=%fused_computation.8 | custom fusion | bytes 790528
  88.0 4.0 gather_fusion.6
  92.0 6.9 %scatter_fusion = bf16[8192,128]{1,0:T(8,128)(2,1)} fusion(bf16[8192,128]{1,0:T(8,128)(2,1)} %bitcast.50, s32[1024]{0:T(1024)S(1)} %broadcast_select_fusion.5, bf16[1024,128]{1,0:T(8,128)(2,1)} %bitcast.6), kind=kCustom, calls=%fused_computation.7 | custom fusion | bytes 790528
  98.9 4.0 gather_fusion.4
  102.9 4.6 broadcast_select_fusion.1
  107.5 8.2 %reshape.510 = bf16[32,256,2,64]{3,2,1,0:T(2,128)(2,1)} reshape(bf16[512,16,128]{2,1,0:T(8,128)(2,1)} %get-tuple-element.22) | data formatting | bytes 4194304 | tf_op jit(solution)/shard_map/reshape | solution.py:77
  115.7 8.3 %reshape.513 = bf16[32,256,2,64]{3,2,1,0:T(2,128)(2,1)} reshape(bf16[512,16,128]{2,1,0:T(8,128)(2,1)} %get-tuple-element.23) | data formatting | bytes 4194304 | tf_op jit(solution)/shard_map/reshape | solution.py:74
  124.0 3.9 reshape.514
  127.9 4.0 fusion.7
  135.8 4.9 fusion.49
  140.7 4.5 convert_bitcast_fusion
  147.7 4.7 reshape.515
  152.4 7.5 %all-to-all-start.3 = ((bf16[32,32,512]{2,1,0:T(8,128)(2,1)}), bf16[32,32,512]{2,1,0:T(8,128)(2,1)S(1)}, u32[]{:S(2)}, u32[]{:S(2)}) async-start(bf16[32,32,512]{2,1,0:T(8,128)(2,1)} %reshape.515), calls=%async_computation.3 | async-start | bytes 2097152 | tf_op jit(solution)/shard_map/all_to_all | solution.py:143
  159.9 16.7 %all-to-all-done.3 = bf16[32,32,512]{2,1,0:T(8,128)(2,1)S(1)} async-done(((bf16[32,32,512]{2,1,0:T(8,128)(2,1)}), bf16[32,32,512]{2,1,0:T(8,128)(2,1)S(1)}, u32[]{:S(2)}, u32[]{:S(2)}) %all-to-all-start.3) | async-done | bytes 1048608 | tf_op jit(solution)/shard_map/all_to_all | solution.py:143
  179.3 3.7 convolution_convert_fusion.1
  183.1 81.3 %all-gather.6.cloned.1.call-done = bf16[2048,2048]{1,0:T(8,128)(2,1)} async-done(((bf16[512,2048]{1,0:T(8,128)(2,1)}), bf16[2048,2048]{1,0:T(8,128)(2,1)}) %all-gather.6.cloned.1.call-update) | async-done | bytes 8388624 | tf_op jit(solution)/shard_map/all_gather | solution.py:146
  264.4 7.2 %reduce_sum.61 = bf16[512,2048]{1,0:T(8,128)(2,1)} reduce(bf16[4,512,2048]{2,1,0:T(8,128)(2,1)} %bitcast.57, bf16[]{:T(256)} %constant.128.clone.1), dimensions={0}, to_apply=%region_8.11 | reduce | flops 3145728 | bytes 10485762 | tf_op jit(solution)/shard_map/reduce_sum | solution.py:146
  275.4 73.7 %all-gather.4.cloned.1.call-done = bf16[4096,2048]{1,0:T(8,128)(2,1)} async-done(((bf16[128,2048]{1,0:T(8,128)(2,1)}), bf16[4096,2048]{1,0:T(8,128)(2,1)}) %all-gather.4.cloned.1.call-update) | async-done | bytes 16777232 | tf_op jit(solution)/shard_map/all_gather | solution.py:154
  349.1 10.4 %fusion.50 = f32[4096,256]{1,0:T(8,128)} fusion(bf16[4096,2048]{1,0:T(8,128)(2,1)} %all-gather.4.cloned.1.call-done, bf16[2048,256]{1,0:T(8,128)(2,1)S(1)} %copy-done.14), kind=kOutput, calls=%fused_computation.133 | convolution fusion | flops 4294967296 | bytes 22020096 | tf_op jit(solution)/shard_map/dot_general | solution.py:155
  359.5 24.7 %convolution_convert_fusion = bf16[4096,2048]{1,0:T(8,128)(2,1)} fusion(bf16[256,2048]{1,0:T(8,128)(2,1)} %param.29, bf16[4096,2048]{1,0:T(8,128)(2,1)} %all-gather.4.cloned.1.call-done, bf16[2048,256]{1,0:T(8,128)(2,1)} %param.28, f32[4096,256]{1,0:T(8,128)} %fusion.50), kind=kOutput, calls=%fused_computation.10 | convolution fusion | flops 8604614656 | bytes 39845888 | tf_op jit(solution)/shard_map/dot_general | solution.py:159
  384.3 114.9 %reduce-scatter.2.cloned.1.call-done = bf16[128,2048]{1,0:T(8,128)(2,1)} async-done(((bf16[4096,2048]{1,0:T(8,128)(2,1)}), bf16[128,2048]{1,0:T(8,128)(2,1)}) %reduce-scatter.2.cloned.1.call-update) | async-done | bytes 524304 | tf_op jit(solution)/shard_map/reduce_scatter | solution.py:158
  (101 shorter events, 34.1 us)
Async XLA Ops:
  7.2 172.1 %copy-start = (bf16[512,2048]{1,0:T(8,128)(2,1)S(1)}, bf16[512,2048]{1,0:T(8,128)(2,1)}, u32[]{:S(2)}) copy-start(bf16[512,2048]{1,0:T(8,128)(2,1)} %param.26) | copy-start | bytes 6291460
  7.2 3.4 copy-start.5
  7.2 4.8 copy-start.8
  10.6 4.0 copy-start.15
  10.6 4.0 copy-start.16
  12.3 4.6 copy-start.2
  18.8 15.9 %copy-start.7 = (s32[1,512]{1,0:T(1,128)S(1)}, s32[1,512]{1,0:T(1,128)}, u32[]{:S(2)}) copy-start(s32[1,512]{1,0:T(1,128)} %param.35) | copy-start | bytes 6148
  18.8 16.0 %copy-start.10 = (s32[1,32]{1,0:T(1,128)S(1)}, s32[1,32]{1,0:T(1,128)}, u32[]{:S(2)}) copy-start(s32[1,32]{1,0:T(1,128)} %param.34) | copy-start | bytes 388
  18.8 17.6 %copy-start.11 = (s32[1,32]{1,0:T(1,128)S(1)}, s32[1,32]{1,0:T(1,128)}, u32[]{:S(2)}) copy-start(s32[1,32]{1,0:T(1,128)} %param.33) | copy-start | bytes 388
  26.3 30.1 %all-to-all-start.1 = ((bf16[32,32,128]{2,1,0:T(8,128)(2,1)}), bf16[32,32,128]{2,1,0:T(8,128)(2,1)S(1)}, u32[]{:S(2)}, u32[]{:S(2)}) async-start(bf16[32,32,128]{2,1,0:T(8,128)(2,1)} %bitcast.10), calls=%async_computation.1 | async-start | bytes 524288 | tf_op jit(solution)/shard_map/all_to_all | solution.py:137
  37.1 7.2 %copy-start.13 = (s32[2]{0:T(128)S(1)}, s32[2]{0:T(128)}, u32[]{:S(2)}) copy-start(s32[2]{0:T(128)} %constant.140) | copy-start | bytes 28
  37.1 7.3 %copy-start.12 = (s32[2]{0:T(128)S(1)}, s32[2]{0:T(128)}, u32[]{:S(2)}) copy-start(s32[2]{0:T(128)} %constant.137) | copy-start | bytes 28
  56.4 16.4 %all-to-all-start = ((bf16[32,32,128]{2,1,0:T(8,128)(2,1)}), bf16[32,32,128]{2,1,0:T(8,128)(2,1)}, u32[]{:S(2)}, u32[]{:S(2)}) async-start(bf16[32,32,128]{2,1,0:T(8,128)(2,1)} %bitcast.5), calls=%async_computation | async-start | bytes 524288 | tf_op jit(solution)/shard_map/all_to_all | solution.py:138
  72.9 51.2 %all-to-all-start.2 = ((bf16[32,32,512]{2,1,0:T(8,128)(2,1)}), bf16[32,32,512]{2,1,0:T(8,128)(2,1)}, u32[]{:S(2)}, u32[]{:S(2)}) async-start(bf16[32,32,512]{2,1,0:T(8,128)(2,1)} %broadcast_select_fusion.2), calls=%async_computation.2 | async-start | bytes 2097152 | tf_op jit(solution)/shard_map/all_to_all | solution.py:136
  115.7 12.2 %copy-start.3 = (f32[32,32,32]{2,1,0:T(8,128)S(1)}, f32[32,32,32]{2,1,0:T(8,128)}, u32[]{:S(2)}) copy-start(f32[32,32,32]{2,1,0:T(8,128)} %get-tuple-element.16) | copy-start | bytes 393220
  131.9 2.2 copy-start.1
  134.1 1.7 copy-start.6
  135.8 4.9 copy-start.4
  152.4 24.3 %all-to-all-start.3 = ((bf16[32,32,512]{2,1,0:T(8,128)(2,1)}), bf16[32,32,512]{2,1,0:T(8,128)(2,1)S(1)}, u32[]{:S(2)}, u32[]{:S(2)}) async-start(bf16[32,32,512]{2,1,0:T(8,128)(2,1)} %reshape.515), calls=%async_computation.3 | async-start | bytes 2097152 | tf_op jit(solution)/shard_map/all_to_all | solution.py:143
  159.8 104.5 %all-gather.6.cloned.1.call-start = ((), (), s32[]{:S(2)}) async-start(), calls=%async_computation.7 | async-start | bytes 10485760 | tf_op jit(solution)/shard_map/all_gather | solution.py:146
  183.0 166.1 %all-gather.4.cloned.1.call-start = ((), (), s32[]{:S(2)}) async-start(), calls=%async_computation.5 | async-start | bytes 17301504 | tf_op jit(solution)/shard_map/all_gather | solution.py:154
  264.4 8.7 %copy-start.9 = (f32[2048]{0:T(1024)S(1)}, f32[2048]{0:T(1024)}, u32[]{:S(2)}) copy-start(f32[2048]{0:T(1024)} %param.22) | copy-start | bytes 24580
  264.4 84.7 %copy-start.14 = (bf16[2048,256]{1,0:T(8,128)(2,1)S(1)}, bf16[2048,256]{1,0:T(8,128)(2,1)}, u32[]{:S(2)}) copy-start(bf16[2048,256]{1,0:T(8,128)(2,1)} %param.27) | copy-start | bytes 3145732
  275.4 223.8 %reduce-scatter.2.cloned.1.call-start = ((), (), s32[]{:S(2)}) async-start(), calls=%async_computation.6 | async-start | bytes 17301504 | tf_op jit(solution)/shard_map/reduce_scatter | solution.py:158
Sparse Core Ops, SparseCore 0:
  183.1 81.1 all-gather.5
  275.5 73.5 all-gather.3
  384.4 114.7 reduce-scatter.1
